TPU v7x, 128 devices: a whole 4x4x4 slice. The times are simulated.
128 devices in a mesh: row: 8 (over y_lo, z), col: 16 (over y_hi, x, core).
Axes of the slice: x: 4, y: 4 (y_hi: 2, y_lo: 2; y = y_hi * 2 + y_lo), z: 4, core: 2. Of those that a mesh axis runs over, the one named last changes fastest.
Arguments:
- embedding: float32 [16384, 256], P(('row', 'col')), may hold values from -6 to 6
- seed_cluster: int32 [16384], P(('row', 'col')), may hold values from 0 to 127
Outputs:
- log_member: float32 [16384, 128], P(('row', 'col'))
All inputs are finite; a program needn't handle non-finite values.
Results may differ from a plain program's by a relative error of at most 0.0003.
Values sent between devices are 32-bit elements; how exact they have to be, the bound alone decides.
No kernel may reach another device: no remote copies, remote signals or barrier semaphores. Data moves between devices by JAX's collectives and lax.ppermute only.
A program may use at most 64 MiB of HBM per device.

v0:
```python
import jax
import jax.numpy as jnp
from jax import lax
from jax.sharding import Mesh
from jax.sharding import PartitionSpec as P

CLUSTER_COUNT = 128
SWEEPS = 2
COL = ("col_0", "col_1", "col_2")
ROW = ("row_0", "row_1")
ROW_COL = ("row_0", "row_1", "col_0", "col_1", "col_2")
ANNEAL_TEMP_VALUE = 0.02


def from_everyone(x, axis):
    copies = jnp.broadcast_to(x, (lax.axis_size(axis), *x.shape))
    return lax.all_to_all(copies, axis, split_axis=0, concat_axis=0, tiled=True)


def in_order(blocks, dim):
    shape = list(blocks.shape[1:])
    shape[dim] *= blocks.shape[0]
    return jnp.moveaxis(blocks, 0, dim).reshape(shape)


def gathered_by_axis(x, axes, dim):
    far, near = axes
    blocks = from_everyone(from_everyone(x, far), near)
    return in_order(blocks.swapaxes(0, 1).reshape(-1, *x.shape), dim)


def gather_directly(x, axis, dim):
    blocks = from_everyone(x, axis)
    return in_order(blocks, dim)


def padded_to(lines, peers):
    spare = -len(lines) % peers
    return jnp.pad(lines, [(0, spare)] + [(0, 0)] * (lines.ndim - 1))


def in_blocks(x, dim, peers):
    before, after = (x.shape[:dim], x.shape[dim + 1 :])
    return jnp.moveaxis(x.reshape(*before, peers, -1, *after), dim, 0)


def sent_and_summed(x, axis, dim):
    peers = lax.axis_size(axis)
    blocks = lax.all_to_all(in_blocks(x, dim, peers), axis, 0, 0, tiled=True)
    return jnp.sum(blocks, axis=0)


def sum_in_two_steps(x, axes, dim):
    far, near = axes
    own = sent_and_summed(in_blocks(x, dim, lax.axis_size(far)), near, dim + 1)
    return jnp.sum(lax.all_to_all(own, far, 0, 0, tiled=True), axis=0)


def total_of(x, axes):
    lines = x.reshape(-1, x.shape[-1])
    padded = padded_to(lines, lax.axis_size(axes[0]) * lax.axis_size(axes[1]))
    whole = gathered_by_axis(sum_in_two_steps(padded, axes, 0), axes, 0)
    return lax.slice_in_dim(whole, 0, len(lines)).reshape(x.shape)


def by_axis(x, axes):
    for axis in axes:
        x = lax.psum(x, axis)
    return x


def shards(embedding, seed_cluster):
    per_device = embedding.shape[0]
    row_coords = gathered_by_axis(embedding, (("col_0", "col_1"), "col_2"), 0)
    col_coords, col_seeds = (
        gather_directly(embedding, ROW, 0),
        gather_directly(seed_cluster, ROW, 0),
    )
    row_sq = jnp.sum(row_coords * row_coords, axis=1)
    col_sq = jnp.sum(col_coords * col_coords, axis=1)
    inner = jnp.dot(row_coords, col_coords.T, precision=lax.Precision.HIGHEST)
    distance = jnp.sqrt(row_sq[:, None] + col_sq[None, :] - 2.0 * inner + 1.0)
    cluster_labels = jnp.arange(CLUSTER_COUNT, dtype=jnp.int32)
    member_cols = (
        0.5 * (col_seeds[:, None] == cluster_labels[None, :]).astype(jnp.float32)
        + 0.5 / CLUSTER_COUNT
    )
    member_own = (
        0.5 * (seed_cluster[:, None] == cluster_labels[None, :]).astype(jnp.float32)
        + 0.5 / CLUSTER_COUNT
    )
    log_member = jnp.zeros((per_device, CLUSTER_COUNT), jnp.float32)
    for sweep in range(SWEEPS):
        columns = member_cols
        summed_weights = total_of(
            jnp.dot(distance, columns, precision=lax.Precision.HIGHEST),
            (("col_0", "col_1"), "col_2"),
        )
        attraction = lax.dynamic_slice_in_dim(
            summed_weights, lax.axis_index(COL) * per_device, per_device, 0
        )
        counts, cohesion = (
            by_axis(jnp.sum(member_own, axis=0), ROW_COL),
            by_axis(jnp.sum(member_own * attraction, axis=0), ROW_COL),
        )
        pair_energy = attraction / counts[None, :] - cohesion[None, :] / (
            2.0 * counts[None, :] ** 2
        )
        member_logits = -pair_energy / ANNEAL_TEMP_VALUE
        highest = jnp.max(member_logits, axis=1, keepdims=True)
        log_member = (
            member_logits
            - highest
            - jnp.log(jnp.sum(jnp.exp(member_logits - highest), axis=1, keepdims=True))
        )
        member_own = jnp.exp(log_member)
        if sweep + 1 < SWEEPS:
            member_cols = gather_directly(member_own, ROW, 0)
    return log_member


def solution(mesh):
    finer = Mesh(mesh.devices.reshape(2, 4, 2, 4, 2), ("row_0", "row_1", "col_0", "col_1", "col_2"))
    placed = (P(ROW_COL, None), P(ROW_COL))
    return jax.shard_map(
        shards, mesh=finer, in_specs=placed, out_specs=P(ROW_COL, None), check_vma=False
    )
```

profile of v0, /device:TPU:1, one launch (start us, length us, event | category | flops | bytes accessed | tf_op | source)
XLA Modules:
  0.0 247.6 jit_solution(4716282031314174073)
XLA Ops:
  0.0 2.0 broadcast_in_dim.16
  2.0 23.8 %all_to_all.66 = f32[8,128,256]{2,1,0:T(8,128)S(1)} all-to-all(f32[8,128,256]{2,1,0:T(8,128)} %broadcast_in_dim.16), channel_id=1, replica_groups=mesh['row_0'=2,'row_1'=4,'col_0'=2,'col_1'=4,'col_2'=2] {'col_0','col_1'}, dimensions={0} | all-to-all | bytes 2097152 | tf_op jit(solution)/shard_map/all_to_all | solution.py:17
  25.8 0.2 broadcast_in_dim.17
  26.0 6.9 %all_to_all.67 = f32[2,8,128,256]{3,2,1,0:T(8,128)S(1)} all-to-all(f32[2,8,128,256]{3,2,1,0:T(8,128)S(1)} %broadcast_in_dim.17), channel_id=1, replica_groups=mesh['row_0'=2,'row_1'=4,'col_0'=2,'col_1'=4,'col_2'=2] {'col_2'}, dimensions={0} | all-to-all | bytes 4194304 | tf_op jit(solution)/shard_map/all_to_all | solution.py:17
  32.9 5.1 %all-to-all-start.2 = ((f32[8,128,256]{2,1,0:T(8,128)}), f32[8,128,256]{2,1,0:T(8,128)S(1)}, u32[]{:S(2)}, u32[]{:S(2)}) async-start(f32[8,128,256]{2,1,0:T(8,128)} %broadcast_in_dim.16), calls=%async_computation.2 | async-start | bytes 2097152 | tf_op jit(solution)/shard_map/all_to_all | solution.py:17
  38.0 1.6 copy.11
  39.7 0.4 fusion
  40.0 13.0 %all-to-all-done.2 = f32[8,128,256]{2,1,0:T(8,128)S(1)} async-done(((f32[8,128,256]{2,1,0:T(8,128)}), f32[8,128,256]{2,1,0:T(8,128)S(1)}, u32[]{:S(2)}, u32[]{:S(2)}) %all-to-all-start.2) | async-done | bytes 1048608 | tf_op jit(solution)/shard_map/all_to_all | solution.py:17
  53.0 0.6 broadcast_in_dim.18
  53.6 3.7 %all-to-all-start.3 = ((s32[8,1,128]{2,1,0:T(1,128)}), s32[8,1,128]{2,1,0:T(1,128)S(1)}, u32[]{:S(2)}, u32[]{:S(2)}) async-start(s32[8,1,128]{2,1,0:T(1,128)} %broadcast_in_dim.18), calls=%async_computation.3 | async-start | bytes 8192 | tf_op jit(solution)/shard_map/all_to_all | solution.py:17
  57.3 0.2 multiply_reduce_fusion
  57.5 13.6 %add_sqrt_fusion = f32[2048,1024]{1,0:T(8,128)} fusion(f32[2048,256]{1,0:T(8,128)} %bitcast.38, f32[1024,256]{1,0:T(8,128)S(1)} %bitcast.35, f32[1024]{0:T(1024)S(1)} %bitcast.50, f32[2048]{0:T(1024)S(1)} %bitcast.49), kind=kOutput, calls=%fused_computation | convolution fusion | flops 6450839552 | bytes 11546624 | tf_op jit(solution)/shard_map/dot_general | solution.py:81
  71.1 9.2 %fusion.1 = f32[2048,128]{1,0:T(8,128)S(1)} fusion(f32[2048,1024]{1,0:T(8,128)} %add_sqrt_fusion, s32[1024]{0:T(1024)S(1)} %bitcast.48), kind=kOutput, calls=%fused_computation.6 | convolution fusion | flops 3221618688 | bytes 9441280 | tf_op jit(solution)/shard_map/dot_general | solution.py:96
  80.3 0.1 copy.19
  80.4 5.0 %all_to_all.68 = f32[2,8,128,128]{3,2,1,0:T(8,128)S(1)} all-to-all(f32[2,8,128,128]{3,2,1,0:T(8,128)S(1)} %bitcast.36), channel_id=1, replica_groups=mesh['row_0'=2,'row_1'=4,'col_0'=2,'col_1'=4,'col_2'=2] {'col_2'}, dimensions={0} | all-to-all | bytes 2097152 | tf_op jit(solution)/shard_map/all_to_all | solution.py:49
  85.3 0.1 reduce_sum.110
  85.4 13.9 %all_to_all.69 = f32[8,128,128]{2,1,0:T(8,128)S(1)} all-to-all(f32[8,128,128]{2,1,0:T(8,128)S(1)} %reduce_sum.110), channel_id=1, replica_groups=mesh['row_0'=2,'row_1'=4,'col_0'=2,'col_1'=4,'col_2'=2] {'col_0','col_1'}, dimensions={0} | all-to-all | bytes 1048576 | tf_op jit(solution)/shard_map/all_to_all | solution.py:56
  99.4 0.9 broadcast_in_dim.19
  100.3 3.5 %all-to-all-start.6 = ((f32[8,128,128]{2,1,0:T(8,128)}), f32[8,128,128]{2,1,0:T(8,128)S(1)}, u32[]{:S(2)}, u32[]{:S(2)}) async-start(f32[8,128,128]{2,1,0:T(8,128)} %broadcast_in_dim.19), calls=%async_computation.6 | async-start | bytes 1048576 | tf_op jit(solution)/shard_map/all_to_all | solution.py:17
  103.8 11.4 %all-to-all-done.6 = f32[8,128,128]{2,1,0:T(8,128)S(1)} async-done(((f32[8,128,128]{2,1,0:T(8,128)}), f32[8,128,128]{2,1,0:T(8,128)S(1)}, u32[]{:S(2)}, u32[]{:S(2)}) %all-to-all-start.6) | async-done | bytes 524320 | tf_op jit(solution)/shard_map/all_to_all | solution.py:17
  115.2 0.1 broadcast_in_dim.20
  115.3 5.3 %all_to_all.70 = f32[2,8,128,128]{3,2,1,0:T(8,128)S(1)} all-to-all(f32[2,8,128,128]{3,2,1,0:T(8,128)S(1)} %broadcast_in_dim.20), channel_id=1, replica_groups=mesh['row_0'=2,'row_1'=4,'col_0'=2,'col_1'=4,'col_2'=2] {'col_2'}, dimensions={0} | all-to-all | bytes 2097152 | tf_op jit(solution)/shard_map/all_to_all | solution.py:17
  120.6 0.1 fusion.8
  120.7 4.3 %all-reduce.9 = (f32[128]{0:T(128)S(1)}, f32[128]{0:T(128)S(1)}) all-reduce(f32[128]{0:T(128)S(1)} %get-tuple-element.8, f32[128]{0:T(128)S(1)} %get-tuple-element.7), channel_id=1, replica_groups=mesh['row_0'=2,'row_1'=4,'col_0'=2,'col_1'=4,'col_2'=2] {'row_0'}, use_global_device_ids=true, to_apply=%region_11.12 | all-reduce | flops 256 | bytes 2048 | tf_op jit(solution)/shard_map/psum | solution.py:68
  125.0 8.4 %all-reduce.3 = (f32[128]{0:T(128)S(1)}, f32[128]{0:T(128)S(1)}) all-reduce(f32[128]{0:T(128)S(1)} %get-tuple-element.27, f32[128]{0:T(128)S(1)} %get-tuple-element.28), channel_id=1, replica_groups=mesh['row_0'=2,'row_1'=4,'col_0'=2,'col_1'=4,'col_2'=2] {'row_1'}, use_global_device_ids=true, to_apply=%region_12.13 | all-reduce | flops 256 | bytes 2048 | tf_op jit(solution)/shard_map/psum | solution.py:68
  133.5 5.3 %all-reduce.7 = (f32[128]{0:T(128)S(1)}, f32[128]{0:T(128)S(1)}) all-reduce(f32[128]{0:T(128)S(1)} %get-tuple-element.15, f32[128]{0:T(128)S(1)} %get-tuple-element.16), channel_id=1, replica_groups=mesh['row_0'=2,'row_1'=4,'col_0'=2,'col_1'=4,'col_2'=2] {'col_0'}, use_global_device_ids=true, to_apply=%region_13.14 | all-reduce | flops 256 | bytes 2048 | tf_op jit(solution)/shard_map/psum | solution.py:68
  138.7 6.6 %all-reduce.1 = (f32[128]{0:T(128)S(1)}, f32[128]{0:T(128)S(1)}) all-reduce(f32[128]{0:T(128)S(1)} %get-tuple-element.23, f32[128]{0:T(128)S(1)} %get-tuple-element.24), channel_id=1, replica_groups=mesh['row_0'=2,'row_1'=4,'col_0'=2,'col_1'=4,'col_2'=2] {'col_1'}, use_global_device_ids=true, to_apply=%region_14.15 | all-reduce | flops 256 | bytes 2048 | tf_op jit(solution)/shard_map/psum | solution.py:68
  145.3 9.0 %all-reduce.5 = (f32[128]{0:T(128)S(1)}, f32[128]{0:T(128)S(1)}) all-reduce(f32[128]{0:T(128)S(1)} %get-tuple-element.11, f32[128]{0:T(128)S(1)} %get-tuple-element.12), channel_id=1, replica_groups=mesh['row_0'=2,'row_1'=4,'col_0'=2,'col_1'=4,'col_2'=2] {'col_2'}, use_global_device_ids=true, to_apply=%region_15.16 | all-reduce | flops 256 | bytes 2048 | tf_op jit(solution)/shard_map/psum | solution.py:68
  154.3 0.1 fusion.12
  154.4 0.2 exponential_reduce_fusion.1
  154.6 0.1 subtract_exponential_fusion
  154.8 11.6 %all_to_all.71 = f32[8,128,128]{2,1,0:T(8,128)S(1)} all-to-all(f32[8,128,128]{2,1,0:T(8,128)S(1)} %broadcast_in_dim.21), channel_id=1, replica_groups=mesh['row_0'=2,'row_1'=4,'col_0'=2,'col_1'=4,'col_2'=2] {'row_0','row_1'}, dimensions={0} | all-to-all | bytes 1048576 | tf_op jit(solution)/shard_map/all_to_all | solution.py:17
  166.4 9.1 %convolution_bitcast_fusion = f32[2,8,128,128]{3,2,0,1:T(8,128)S(1)} fusion(f32[8,2,128,1024]{3,2,1,0:T(8,128)} %bitcast.33, f32[1024,128,1,1]{1,0,3,2:T(8,128)S(1)} %bitcast.37), kind=kOutput, calls=%fused_computation.3 | convolution fusion | flops 3221225472 | bytes 9961472 | tf_op jit(solution)/shard_map/dot_general | solution.py:96
  175.6 6.4 %all_to_all.72 = f32[2,8,128,128]{3,2,1,0:T(8,128)S(1)} all-to-all(f32[2,8,128,128]{3,2,1,0:T(8,128)S(1)} %copy.14), channel_id=1, replica_groups=mesh['row_0'=2,'row_1'=4,'col_0'=2,'col_1'=4,'col_2'=2] {'col_2'}, dimensions={0} | all-to-all | bytes 2097152 | tf_op jit(solution)/shard_map/all_to_all | solution.py:49
  181.9 0.1 reduce_sum.115
  182.0 13.8 %all_to_all.73 = f32[8,128,128]{2,1,0:T(8,128)S(1)} all-to-all(f32[8,128,128]{2,1,0:T(8,128)S(1)} %reduce_sum.115), channel_id=1, replica_groups=mesh['row_0'=2,'row_1'=4,'col_0'=2,'col_1'=4,'col_2'=2] {'col_0','col_1'}, dimensions={0} | all-to-all | bytes 1048576 | tf_op jit(solution)/shard_map/all_to_all | solution.py:56
  195.9 12.7 %all_to_all.74 = f32[8,128,128]{2,1,0:T(8,128)S(1)} all-to-all(f32[8,128,128]{2,1,0:T(8,128)S(1)} %broadcast_in_dim.22), channel_id=1, replica_groups=mesh['row_0'=2,'row_1'=4,'col_0'=2,'col_1'=4,'col_2'=2] {'col_0','col_1'}, dimensions={0} | all-to-all | bytes 1048576 | tf_op jit(solution)/shard_map/all_to_all | solution.py:17
  208.7 0.1 broadcast_in_dim.23
  208.8 6.4 %all_to_all.75 = f32[2,8,128,128]{3,2,1,0:T(8,128)S(1)} all-to-all(f32[2,8,128,128]{3,2,1,0:T(8,128)S(1)} %broadcast_in_dim.23), channel_id=1, replica_groups=mesh['row_0'=2,'row_1'=4,'col_0'=2,'col_1'=4,'col_2'=2] {'col_2'}, dimensions={0} | all-to-all | bytes 2097152 | tf_op jit(solution)/shard_map/all_to_all | solution.py:17
  215.2 0.1 fusion.14
  215.4 3.8 %all-reduce.8 = (f32[128]{0:T(128)S(1)}, f32[128]{0:T(128)S(1)}) all-reduce(f32[128]{0:T(128)S(1)} %get-tuple-element.6, f32[128]{0:T(128)S(1)} %get-tuple-element.5), channel_id=1, replica_groups=mesh['row_0'=2,'row_1'=4,'col_0'=2,'col_1'=4,'col_2'=2] {'row_0'}, use_global_device_ids=true, to_apply=%region_27.28 | all-reduce | flops 256 | bytes 2048 | tf_op jit(solution)/shard_map/psum | solution.py:68
  219.2 6.5 %all-reduce.2 = (f32[128]{0:T(128)S(1)}, f32[128]{0:T(128)S(1)}) all-reduce(f32[128]{0:T(128)S(1)} %get-tuple-element.25, f32[128]{0:T(128)S(1)} %get-tuple-element.26), channel_id=1, replica_groups=mesh['row_0'=2,'row_1'=4,'col_0'=2,'col_1'=4,'col_2'=2] {'row_1'}, use_global_device_ids=true, to_apply=%region_28.29 | all-reduce | flops 256 | bytes 2048 | tf_op jit(solution)/shard_map/psum | solution.py:68
  225.7 5.3 %all-reduce.6 = (f32[128]{0:T(128)S(1)}, f32[128]{0:T(128)S(1)}) all-reduce(f32[128]{0:T(128)S(1)} %get-tuple-element.13, f32[128]{0:T(128)S(1)} %get-tuple-element.14), channel_id=1, replica_groups=mesh['row_0'=2,'row_1'=4,'col_0'=2,'col_1'=4,'col_2'=2] {'col_0'}, use_global_device_ids=true, to_apply=%region_29.30 | all-reduce | flops 256 | bytes 2048 | tf_op jit(solution)/shard_map/psum | solution.py:68
  230.9 6.8 %all-reduce = (f32[128]{0:T(128)S(1)}, f32[128]{0:T(128)S(1)}) all-reduce(f32[128]{0:T(128)S(1)} %get-tuple-element.21, f32[128]{0:T(128)S(1)} %get-tuple-element.22), channel_id=1, replica_groups=mesh['row_0'=2,'row_1'=4,'col_0'=2,'col_1'=4,'col_2'=2] {'col_1'}, use_global_device_ids=true, to_apply=%region_30.31 | all-reduce | flops 256 | bytes 2048 | tf_op jit(solution)/shard_map/psum | solution.py:68
  237.7 8.8 %all-reduce.4 = (f32[128]{0:T(128)S(1)}, f32[128]{0:T(128)S(1)}) all-reduce(f32[128]{0:T(128)S(1)} %get-tuple-element.9, f32[128]{0:T(128)S(1)} %get-tuple-element.10), channel_id=1, replica_groups=mesh['row_0'=2,'row_1'=4,'col_0'=2,'col_1'=4,'col_2'=2] {'col_2'}, use_global_device_ids=true, to_apply=%region_31.32 | all-reduce | flops 256 | bytes 2048 | tf_op jit(solution)/shard_map/psum | solution.py:68
  246.6 0.1 fusion.13
  246.7 0.2 exponential_reduce_fusion
  246.9 0.7 subtract_subtract_fusion
  (14 shorter events, 0.4 us)
Async XLA Ops:
  25.8 27.2 %copy-start = (s32[128]{0:T(128)S(1)}, s32[128]{0:T(128)}, u32[]{:S(2)}) copy-start(s32[128]{0:T(128)} %param.3) | copy-start | bytes 1540
  32.9 20.1 %all-to-all-start.2 = ((f32[8,128,256]{2,1,0:T(8,128)}), f32[8,128,256]{2,1,0:T(8,128)S(1)}, u32[]{:S(2)}, u32[]{:S(2)}) async-start(f32[8,128,256]{2,1,0:T(8,128)} %broadcast_in_dim.16), calls=%async_computation.2 | async-start | bytes 2097152 | tf_op jit(solution)/shard_map/all_to_all | solution.py:17
  53.6 17.5 %all-to-all-start.3 = ((s32[8,1,128]{2,1,0:T(1,128)}), s32[8,1,128]{2,1,0:T(1,128)S(1)}, u32[]{:S(2)}, u32[]{:S(2)}) async-start(s32[8,1,128]{2,1,0:T(1,128)} %broadcast_in_dim.18), calls=%async_computation.3 | async-start | bytes 8192 | tf_op jit(solution)/shard_map/all_to_all | solution.py:17
  100.3 14.9 %all-to-all-start.6 = ((f32[8,128,128]{2,1,0:T(8,128)}), f32[8,128,128]{2,1,0:T(8,128)S(1)}, u32[]{:S(2)}, u32[]{:S(2)}) async-start(f32[8,128,128]{2,1,0:T(8,128)} %broadcast_in_dim.19), calls=%async_computation.6 | async-start | bytes 1048576 | tf_op jit(solution)/shard_map/all_to_all | solution.py:17
where the time goes:
time: 249 us; the launch traced here: 248 us
  blocking collectives  170 us (68%)
  matrix products  31.9 us (13%)
  waiting for transfers between devices  24.4 us (10%)
  starting transfers between devices  12.3 us (5%)
  local copies, waits for them, and re-layouts  5.86 us (2%)
  other arithmetic  2.54 us (1%)
    all_to_all x6, blocking collectives, from_everyone(): return lax.all_to_all(copies, axis, split_axis=0, concat_axis=0, tiled=True)  66.7 us
    psum x10, blocking collectives, by_axis(): x = lax.psum(x, axis)  64.7 us
    all_to_all x2, blocking collectives, sum_in_two_steps(): return jnp.sum(lax.all_to_all(own, far, 0, 0, tiled=True), axis=0)  27.7 us
    all_to_all x3, waiting for transfers between devices, from_everyone(): return lax.all_to_all(copies, axis, split_axis=0, concat_axis=0, tiled=True)  24.4 us
    dot_general x2, matrix products, shards(): jnp.dot(distance, columns, precision=lax.Precision.HIGHEST)  18.3 us
    dot_general x1, matrix products, shards(): inner = jnp.dot(row_coords, col_coords.T, precision=lax.Precision.HIGHEST)  13.6 us
    all_to_all x3, starting transfers between devices, from_everyone(): return lax.all_to_all(copies, axis, split_axis=0, concat_axis=0, tiled=True)  12.3 us
    all_to_all x2, blocking collectives, sent_and_summed(): blocks = lax.all_to_all(in_blocks(x, dim, peers), axis, 0, 0, tiled=True)  11.3 us
  transfers between devices with their start and end apart: 3, of which 2 were waited for; matrix products, arithmetic and copies ran while one was open for 6% of the time, Pallas kernels for 0%

commit v1 on v0

--- a/solution.py
+++ b/solution.py
@@ -65,7 +65,8 @@
 
 def by_axis(x, axes):
     for axis in axes:
-        x = lax.psum(x, axis)
+        parts = lax.all_gather(x, axis)
+        x = jnp.sum(parts, axis=0)
     return x
 
 

time: 249 us -> 297 us (1.19)
  blocking collectives: 170 us -> 219 us
    all_gather x0 -> x20, blocking collectives: none -> 112 us  [by_axis(): parts = lax.all_gather(x, axis)]
    psum x10 -> x0, blocking collectives: 64.7 us -> none  [by_axis(): x = lax.psum(x, axis)]
  transfers between devices with their start and end apart: 3 -> 3, of which waited for: 2 -> 2; matrix products, arithmetic and copies ran while one was open for 6% -> 5% of each run, Pallas kernels for 0% -> 0%
where the time goes in v1:
time: 297 us; the launch traced here: 296 us
  blocking collectives  219 us (74%)
  matrix products  31.9 us (11%)
  waiting for transfers between devices  24.4 us (8%)
  starting transfers between devices  12.3 us (4%)
  local copies, waits for them, and re-layouts  5.86 us (2%)
    all_gather x20, blocking collectives, by_axis(): parts = lax.all_gather(x, axis)  112 us
    all_to_all x6, blocking collectives, from_everyone(): return lax.all_to_all(copies, axis, split_axis=0, concat_axis=0, tiled=True)  67.8 us
    all_to_all x2, blocking collectives, sum_in_two_steps(): return jnp.sum(lax.all_to_all(own, far, 0, 0, tiled=True), axis=0)  27.7 us
    all_to_all x3, waiting for transfers between devices, from_everyone(): return lax.all_to_all(copies, axis, split_axis=0, concat_axis=0, tiled=True)  24.4 us
    dot_general x2, matrix products, shards(): jnp.dot(distance, columns, precision=lax.Precision.HIGHEST)  18.3 us
    dot_general x1, matrix products, shards(): inner = jnp.dot(row_coords, col_coords.T, precision=lax.Precision.HIGHEST)  13.6 us
    all_to_all x3, starting transfers between devices, from_everyone(): return lax.all_to_all(copies, axis, split_axis=0, concat_axis=0, tiled=True)  12.3 us
    all_to_all x2, blocking collectives, sent_and_summed(): blocks = lax.all_to_all(in_blocks(x, dim, peers), axis, 0, 0, tiled=True)  11.4 us
  transfers between devices with their start and end apart: 3, of which 2 were waited for; matrix products, arithmetic and copies ran while one was open for 5% of the time, Pallas kernels for 0%

profile of v1, /device:TPU:1, one launch (start us, length us, event | category | flops | bytes accessed | tf_op | source)
XLA Modules:
  0.0 296.1 jit_solution(1828818264624240424)
XLA Ops:
  0.0 2.0 broadcast_in_dim.16
  2.0 23.8 %all_to_all.66 = f32[8,128,256]{2,1,0:T(8,128)S(1)} all-to-all(f32[8,128,256]{2,1,0:T(8,128)} %broadcast_in_dim.16), channel_id=1, replica_groups=mesh['row_0'=2,'row_1'=4,'col_0'=2,'col_1'=4,'col_2'=2] {'col_0','col_1'}, dimensions={0} | all-to-all | bytes 2097152 | tf_op jit(solution)/shard_map/all_to_all | solution.py:17
  25.8 0.2 broadcast_in_dim.17
  26.0 6.9 %all_to_all.67 = f32[2,8,128,256]{3,2,1,0:T(8,128)S(1)} all-to-all(f32[2,8,128,256]{3,2,1,0:T(8,128)S(1)} %broadcast_in_dim.17), channel_id=1, replica_groups=mesh['row_0'=2,'row_1'=4,'col_0'=2,'col_1'=4,'col_2'=2] {'col_2'}, dimensions={0} | all-to-all | bytes 4194304 | tf_op jit(solution)/shard_map/all_to_all | solution.py:17
  32.9 5.1 %all-to-all-start.2 = ((f32[8,128,256]{2,1,0:T(8,128)}), f32[8,128,256]{2,1,0:T(8,128)S(1)}, u32[]{:S(2)}, u32[]{:S(2)}) async-start(f32[8,128,256]{2,1,0:T(8,128)} %broadcast_in_dim.16), calls=%async_computation.2 | async-start | bytes 2097152 | tf_op jit(solution)/shard_map/all_to_all | solution.py:17
  38.0 1.6 copy.11
  39.7 0.4 fusion
  40.0 13.0 %all-to-all-done.2 = f32[8,128,256]{2,1,0:T(8,128)S(1)} async-done(((f32[8,128,256]{2,1,0:T(8,128)}), f32[8,128,256]{2,1,0:T(8,128)S(1)}, u32[]{:S(2)}, u32[]{:S(2)}) %all-to-all-start.2) | async-done | bytes 1048608 | tf_op jit(solution)/shard_map/all_to_all | solution.py:17
  53.0 0.6 broadcast_in_dim.18
  53.6 3.7 %all-to-all-start.3 = ((s32[8,1,128]{2,1,0:T(1,128)}), s32[8,1,128]{2,1,0:T(1,128)S(1)}, u32[]{:S(2)}, u32[]{:S(2)}) async-start(s32[8,1,128]{2,1,0:T(1,128)} %broadcast_in_dim.18), calls=%async_computation.3 | async-start | bytes 8192 | tf_op jit(solution)/shard_map/all_to_all | solution.py:17
  57.3 0.2 multiply_reduce_fusion
  57.5 13.6 %add_sqrt_fusion = f32[2048,1024]{1,0:T(8,128)} fusion(f32[2048,256]{1,0:T(8,128)} %bitcast.58, f32[1024,256]{1,0:T(8,128)S(1)} %bitcast.55, f32[1024]{0:T(1024)S(1)} %bitcast.70, f32[2048]{0:T(1024)S(1)} %bitcast.69), kind=kOutput, calls=%fused_computation | convolution fusion | flops 6450839552 | bytes 11546624 | tf_op jit(solution)/shard_map/dot_general | solution.py:82
  71.1 9.2 %fusion.1 = f32[2048,128]{1,0:T(8,128)S(1)} fusion(f32[2048,1024]{1,0:T(8,128)} %add_sqrt_fusion, s32[1024]{0:T(1024)S(1)} %bitcast.68), kind=kOutput, calls=%fused_computation.6 | convolution fusion | flops 3221618688 | bytes 9441280 | tf_op jit(solution)/shard_map/dot_general | solution.py:97
  80.4 5.0 %all_to_all.68 = f32[2,8,128,128]{3,2,1,0:T(8,128)S(1)} all-to-all(f32[2,8,128,128]{3,2,1,0:T(8,128)S(1)} %bitcast.56), channel_id=1, replica_groups=mesh['row_0'=2,'row_1'=4,'col_0'=2,'col_1'=4,'col_2'=2] {'col_2'}, dimensions={0} | all-to-all | bytes 2097152 | tf_op jit(solution)/shard_map/all_to_all | solution.py:49
  85.4 13.9 %all_to_all.69 = f32[8,128,128]{2,1,0:T(8,128)S(1)} all-to-all(f32[8,128,128]{2,1,0:T(8,128)S(1)} %reduce_sum.290), channel_id=1, replica_groups=mesh['row_0'=2,'row_1'=4,'col_0'=2,'col_1'=4,'col_2'=2] {'col_0','col_1'}, dimensions={0} | all-to-all | bytes 1048576 | tf_op jit(solution)/shard_map/all_to_all | solution.py:56
  99.4 0.9 broadcast_in_dim.19
  100.3 3.5 %all-to-all-start.6 = ((f32[8,128,128]{2,1,0:T(8,128)}), f32[8,128,128]{2,1,0:T(8,128)S(1)}, u32[]{:S(2)}, u32[]{:S(2)}) async-start(f32[8,128,128]{2,1,0:T(8,128)} %broadcast_in_dim.19), calls=%async_computation.6 | async-start | bytes 1048576 | tf_op jit(solution)/shard_map/all_to_all | solution.py:17
  103.8 11.4 %all-to-all-done.6 = f32[8,128,128]{2,1,0:T(8,128)S(1)} async-done(((f32[8,128,128]{2,1,0:T(8,128)}), f32[8,128,128]{2,1,0:T(8,128)S(1)}, u32[]{:S(2)}, u32[]{:S(2)}) %all-to-all-start.6) | async-done | bytes 524320 | tf_op jit(solution)/shard_map/all_to_all | solution.py:17
  115.3 5.3 %all_to_all.70 = f32[2,8,128,128]{3,2,1,0:T(8,128)S(1)} all-to-all(f32[2,8,128,128]{3,2,1,0:T(8,128)S(1)} %broadcast_in_dim.20), channel_id=1, replica_groups=mesh['row_0'=2,'row_1'=4,'col_0'=2,'col_1'=4,'col_2'=2] {'col_2'}, dimensions={0} | all-to-all | bytes 2097152 | tf_op jit(solution)/shard_map/all_to_all | solution.py:17
  120.7 3.6 %all-gather.25 = f32[2,1,128]{2,1,0:T(1,128)S(1)} all-gather(f32[1,1,128]{2,1,0:T(1,128)S(1)} %bitcast.82), channel_id=7, replica_groups=mesh['row_0'=2,'row_1'=4,'col_0'=2,'col_1'=4,'col_2'=2] {'row_0'}, dimensions={0}, use_global_device_ids=true | all-gather | bytes 1536 | tf_op jit(solution)/shard_map/all_gather | solution.py:68
  124.3 7.6 %all-gather.26 = f32[4,1,128]{2,1,0:T(1,128)S(1)} all-gather(f32[1,1,128]{2,1,0:T(1,128)S(1)} %bitcast.71), channel_id=8, replica_groups=mesh['row_0'=2,'row_1'=4,'col_0'=2,'col_1'=4,'col_2'=2] {'row_1'}, dimensions={0}, use_global_device_ids=true | all-gather | bytes 2560 | tf_op jit(solution)/shard_map/all_gather | solution.py:68
  132.0 4.6 %all-gather.27 = f32[2,1,128]{2,1,0:T(1,128)S(1)} all-gather(f32[1,1,128]{2,1,0:T(1,128)S(1)} %bitcast.83), channel_id=9, replica_groups=mesh['row_0'=2,'row_1'=4,'col_0'=2,'col_1'=4,'col_2'=2] {'col_0'}, dimensions={0}, use_global_device_ids=true | all-gather | bytes 1536 | tf_op jit(solution)/shard_map/all_gather | solution.py:68
  136.6 5.8 %all-gather.28 = f32[4,1,128]{2,1,0:T(1,128)S(1)} all-gather(f32[1,1,128]{2,1,0:T(1,128)S(1)} %bitcast.72), channel_id=10, replica_groups=mesh['row_0'=2,'row_1'=4,'col_0'=2,'col_1'=4,'col_2'=2] {'col_1'}, dimensions={0}, use_global_device_ids=true | all-gather | bytes 2560 | tf_op jit(solution)/shard_map/all_gather | solution.py:68
  142.4 8.2 %all-gather.29 = f32[2,1,128]{2,1,0:T(1,128)S(1)} all-gather(f32[1,1,128]{2,1,0:T(1,128)S(1)} %bitcast.84), channel_id=11, replica_groups=mesh['row_0'=2,'row_1'=4,'col_0'=2,'col_1'=4,'col_2'=2] {'col_2'}, dimensions={0}, use_global_device_ids=true | all-gather | bytes 1536 | tf_op jit(solution)/shard_map/all_gather | solution.py:68
  150.6 3.1 %all-gather.20 = f32[2,1,128]{2,1,0:T(1,128)S(1)} all-gather(f32[1,1,128]{2,1,0:T(1,128)S(1)} %bitcast.80), channel_id=2, replica_groups=mesh['row_0'=2,'row_1'=4,'col_0'=2,'col_1'=4,'col_2'=2] {'row_0'}, dimensions={0}, use_global_device_ids=true | all-gather | bytes 1536 | tf_op jit(solution)/shard_map/all_gather | solution.py:68
  153.6 5.2 %all-gather.21 = f32[4,1,128]{2,1,0:T(1,128)S(1)} all-gather(f32[1,1,128]{2,1,0:T(1,128)S(1)} %bitcast.73), channel_id=3, replica_groups=mesh['row_0'=2,'row_1'=4,'col_0'=2,'col_1'=4,'col_2'=2] {'row_1'}, dimensions={0}, use_global_device_ids=true | all-gather | bytes 2560 | tf_op jit(solution)/shard_map/all_gather | solution.py:68
  158.8 4.6 %all-gather.22 = f32[2,1,128]{2,1,0:T(1,128)S(1)} all-gather(f32[1,1,128]{2,1,0:T(1,128)S(1)} %bitcast.85), channel_id=4, replica_groups=mesh['row_0'=2,'row_1'=4,'col_0'=2,'col_1'=4,'col_2'=2] {'col_0'}, dimensions={0}, use_global_device_ids=true | all-gather | bytes 1536 | tf_op jit(solution)/shard_map/all_gather | solution.py:68
  163.4 6.0 %all-gather.23 = f32[4,1,128]{2,1,0:T(1,128)S(1)} all-gather(f32[1,1,128]{2,1,0:T(1,128)S(1)} %bitcast.74), channel_id=5, replica_groups=mesh['row_0'=2,'row_1'=4,'col_0'=2,'col_1'=4,'col_2'=2] {'col_1'}, dimensions={0}, use_global_device_ids=true | all-gather | bytes 2560 | tf_op jit(solution)/shard_map/all_gather | solution.py:68
  169.5 8.0 %all-gather.24 = f32[2,1,128]{2,1,0:T(1,128)S(1)} all-gather(f32[1,1,128]{2,1,0:T(1,128)S(1)} %bitcast.86), channel_id=6, replica_groups=mesh['row_0'=2,'row_1'=4,'col_0'=2,'col_1'=4,'col_2'=2] {'col_2'}, dimensions={0}, use_global_device_ids=true | all-gather | bytes 1536 | tf_op jit(solution)/shard_map/all_gather | solution.py:68
  177.6 0.2 exponential_reduce_fusion.1
  178.0 12.7 %all_to_all.71 = f32[8,128,128]{2,1,0:T(8,128)S(1)} all-to-all(f32[8,128,128]{2,1,0:T(8,128)S(1)} %broadcast_in_dim.21), channel_id=1, replica_groups=mesh['row_0'=2,'row_1'=4,'col_0'=2,'col_1'=4,'col_2'=2] {'row_0','row_1'}, dimensions={0} | all-to-all | bytes 1048576 | tf_op jit(solution)/shard_map/all_to_all | solution.py:17
  190.7 9.1 %convolution_bitcast_fusion = f32[2,8,128,128]{3,2,0,1:T(8,128)S(1)} fusion(f32[8,2,128,1024]{3,2,1,0:T(8,128)} %bitcast.53, f32[1024,128,1,1]{1,0,3,2:T(8,128)S(1)} %bitcast.57), kind=kOutput, calls=%fused_computation.3 | convolution fusion | flops 3221225472 | bytes 9961472 | tf_op jit(solution)/shard_map/dot_general | solution.py:97
  199.8 6.4 %all_to_all.72 = f32[2,8,128,128]{3,2,1,0:T(8,128)S(1)} all-to-all(f32[2,8,128,128]{3,2,1,0:T(8,128)S(1)} %copy.14), channel_id=1, replica_groups=mesh['row_0'=2,'row_1'=4,'col_0'=2,'col_1'=4,'col_2'=2] {'col_2'}, dimensions={0} | all-to-all | bytes 2097152 | tf_op jit(solution)/shard_map/all_to_all | solution.py:49
  206.4 13.8 %all_to_all.73 = f32[8,128,128]{2,1,0:T(8,128)S(1)} all-to-all(f32[8,128,128]{2,1,0:T(8,128)S(1)} %reduce_sum.305), channel_id=1, replica_groups=mesh['row_0'=2,'row_1'=4,'col_0'=2,'col_1'=4,'col_2'=2] {'col_0','col_1'}, dimensions={0} | all-to-all | bytes 1048576 | tf_op jit(solution)/shard_map/all_to_all | solution.py:56
  220.3 12.7 %all_to_all.74 = f32[8,128,128]{2,1,0:T(8,128)S(1)} all-to-all(f32[8,128,128]{2,1,0:T(8,128)S(1)} %broadcast_in_dim.22), channel_id=1, replica_groups=mesh['row_0'=2,'row_1'=4,'col_0'=2,'col_1'=4,'col_2'=2] {'col_0','col_1'}, dimensions={0} | all-to-all | bytes 1048576 | tf_op jit(solution)/shard_map/all_to_all | solution.py:17
  233.1 6.4 %all_to_all.75 = f32[2,8,128,128]{3,2,1,0:T(8,128)S(1)} all-to-all(f32[2,8,128,128]{3,2,1,0:T(8,128)S(1)} %broadcast_in_dim.23), channel_id=1, replica_groups=mesh['row_0'=2,'row_1'=4,'col_0'=2,'col_1'=4,'col_2'=2] {'col_2'}, dimensions={0} | all-to-all | bytes 2097152 | tf_op jit(solution)/shard_map/all_to_all | solution.py:17
  239.7 3.1 %all-gather.35 = f32[2,1,128]{2,1,0:T(1,128)S(1)} all-gather(f32[1,1,128]{2,1,0:T(1,128)S(1)} %bitcast.81), channel_id=17, replica_groups=mesh['row_0'=2,'row_1'=4,'col_0'=2,'col_1'=4,'col_2'=2] {'row_0'}, dimensions={0}, use_global_device_ids=true | all-gather | bytes 1536 | tf_op jit(solution)/shard_map/all_gather | solution.py:68
  242.8 5.7 %all-gather.36 = f32[4,1,128]{2,1,0:T(1,128)S(1)} all-gather(f32[1,1,128]{2,1,0:T(1,128)S(1)} %bitcast.75), channel_id=18, replica_groups=mesh['row_0'=2,'row_1'=4,'col_0'=2,'col_1'=4,'col_2'=2] {'row_1'}, dimensions={0}, use_global_device_ids=true | all-gather | bytes 2560 | tf_op jit(solution)/shard_map/all_gather | solution.py:68
  248.5 4.6 %all-gather.37 = f32[2,1,128]{2,1,0:T(1,128)S(1)} all-gather(f32[1,1,128]{2,1,0:T(1,128)S(1)} %bitcast.87), channel_id=19, replica_groups=mesh['row_0'=2,'row_1'=4,'col_0'=2,'col_1'=4,'col_2'=2] {'col_0'}, dimensions={0}, use_global_device_ids=true | all-gather | bytes 1536 | tf_op jit(solution)/shard_map/all_gather | solution.py:68
  253.1 6.0 %all-gather.38 = f32[4,1,128]{2,1,0:T(1,128)S(1)} all-gather(f32[1,1,128]{2,1,0:T(1,128)S(1)} %bitcast.76), channel_id=20, replica_groups=mesh['row_0'=2,'row_1'=4,'col_0'=2,'col_1'=4,'col_2'=2] {'col_1'}, dimensions={0}, use_global_device_ids=true | all-gather | bytes 2560 | tf_op jit(solution)/shard_map/all_gather | solution.py:68
  259.1 8.2 %all-gather.39 = f32[2,1,128]{2,1,0:T(1,128)S(1)} all-gather(f32[1,1,128]{2,1,0:T(1,128)S(1)} %bitcast.88), channel_id=21, replica_groups=mesh['row_0'=2,'row_1'=4,'col_0'=2,'col_1'=4,'col_2'=2] {'col_2'}, dimensions={0}, use_global_device_ids=true | all-gather | bytes 1536 | tf_op jit(solution)/shard_map/all_gather | solution.py:68
  267.3 3.1 %all-gather.30 = f32[2,1,128]{2,1,0:T(1,128)S(1)} all-gather(f32[1,1,128]{2,1,0:T(1,128)S(1)} %bitcast.79), channel_id=12, replica_groups=mesh['row_0'=2,'row_1'=4,'col_0'=2,'col_1'=4,'col_2'=2] {'row_0'}, dimensions={0}, use_global_device_ids=true | all-gather | bytes 1536 | tf_op jit(solution)/shard_map/all_gather | solution.py:68
  270.4 6.1 %all-gather.31 = f32[4,1,128]{2,1,0:T(1,128)S(1)} all-gather(f32[1,1,128]{2,1,0:T(1,128)S(1)} %bitcast.77), channel_id=13, replica_groups=mesh['row_0'=2,'row_1'=4,'col_0'=2,'col_1'=4,'col_2'=2] {'row_1'}, dimensions={0}, use_global_device_ids=true | all-gather | bytes 2560 | tf_op jit(solution)/shard_map/all_gather | solution.py:68
  276.5 4.6 %all-gather.32 = f32[2,1,128]{2,1,0:T(1,128)S(1)} all-gather(f32[1,1,128]{2,1,0:T(1,128)S(1)} %bitcast.89), channel_id=14, replica_groups=mesh['row_0'=2,'row_1'=4,'col_0'=2,'col_1'=4,'col_2'=2] {'col_0'}, dimensions={0}, use_global_device_ids=true | all-gather | bytes 1536 | tf_op jit(solution)/shard_map/all_gather | solution.py:68
  281.1 5.8 %all-gather.33 = f32[4,1,128]{2,1,0:T(1,128)S(1)} all-gather(f32[1,1,128]{2,1,0:T(1,128)S(1)} %bitcast.78), channel_id=15, replica_groups=mesh['row_0'=2,'row_1'=4,'col_0'=2,'col_1'=4,'col_2'=2] {'col_1'}, dimensions={0}, use_global_device_ids=true | all-gather | bytes 2560 | tf_op jit(solution)/shard_map/all_gather | solution.py:68
  286.9 8.1 %all-gather.34 = f32[2,1,128]{2,1,0:T(1,128)S(1)} all-gather(f32[1,1,128]{2,1,0:T(1,128)S(1)} %bitcast.90), channel_id=16, replica_groups=mesh['row_0'=2,'row_1'=4,'col_0'=2,'col_1'=4,'col_2'=2] {'col_2'}, dimensions={0}, use_global_device_ids=true | all-gather | bytes 1536 | tf_op jit(solution)/shard_map/all_gather | solution.py:68
  295.2 0.2 exponential_reduce_fusion
  295.4 0.7 subtract_subtract_fusion
  (44 shorter events, 1.9 us)
Async XLA Ops:
  25.8 27.2 %copy-start = (s32[128]{0:T(128)S(1)}, s32[128]{0:T(128)}, u32[]{:S(2)}) copy-start(s32[128]{0:T(128)} %param.3) | copy-start | bytes 1540
  32.9 20.1 %all-to-all-start.2 = ((f32[8,128,256]{2,1,0:T(8,128)}), f32[8,128,256]{2,1,0:T(8,128)S(1)}, u32[]{:S(2)}, u32[]{:S(2)}) async-start(f32[8,128,256]{2,1,0:T(8,128)} %broadcast_in_dim.16), calls=%async_computation.2 | async-start | bytes 2097152 | tf_op jit(solution)/shard_map/all_to_all | solution.py:17
  53.6 17.5 %all-to-all-start.3 = ((s32[8,1,128]{2,1,0:T(1,128)}), s32[8,1,128]{2,1,0:T(1,128)S(1)}, u32[]{:S(2)}, u32[]{:S(2)}) async-start(s32[8,1,128]{2,1,0:T(1,128)} %broadcast_in_dim.18), calls=%async_computation.3 | async-start | bytes 8192 | tf_op jit(solution)/shard_map/all_to_all | solution.py:17
  100.3 14.9 %all-to-all-start.6 = ((f32[8,128,128]{2,1,0:T(8,128)}), f32[8,128,128]{2,1,0:T(8,128)S(1)}, u32[]{:S(2)}, u32[]{:S(2)}) async-start(f32[8,128,128]{2,1,0:T(8,128)} %broadcast_in_dim.19), calls=%async_computation.6 | async-start | bytes 1048576 | tf_op jit(solution)/shard_map/all_to_all | solution.py:17
